TPU v7x, 32 devices: a whole 2x2x4 slice. The times are simulated.
32 devices in a mesh: seq: 2 (over x), tok: 16 (over z, y, core).
Axes of the slice: x: 2, y: 2, z: 4, core: 2. Of those that a mesh axis runs over, the one named last changes fastest.
Arguments:
- queries: bfloat16 [8192, 4096], P(('seq', 'tok')), parts along dimension 0, may hold values from -6 to 6
- keys: bfloat16 [8192, 4096], P(('seq', 'tok')), parts along dimension 0, may hold values from -6 to 6
- values: bfloat16 [8192, 4096], P(('seq', 'tok')), parts along dimension 0, may hold values from -6 to 6
- segments: int32 [8192], P(('seq', 'tok')), parts along dimension 0, may hold values from 0 to 31, never falling along the last dimension, each value on 1 to 256 neighbouring positions
- short_filters: bfloat16 [3, 3, 4096], replicated, may hold values from -3.5 to 3.5
- mr_filter: bfloat16 [128, 256], replicated, may hold values from -0.5 to 0.5
- mr_bias: bfloat16 [4096], replicated, may hold values from -1 to 1
Outputs:
- mixed: bfloat16 [8192, 4096], P(('seq', 'tok')), parts along dimension 0
There are 2 independent parts, one for each index of `seq`. A program takes and returns all parts, laid end to end along the dimension named above; an argument that names none is the same for every part. Nothing has to cross between parts.
Inputs may be any that keep to these rules, and one draw needn't show every extreme that they name: `segments`: document numbers never fall along the window; each document spans 1 to 256 positions, and one spans exactly 256.
All inputs are finite; a program needn't handle non-finite values.
Results may differ from a plain program's by a relative error of at most 0.0049.
Values may be sent and summed in bfloat16 or wider, within the bound.
A program may use at most 128 MiB of HBM per device.

v0:
```python
import jax
import jax.numpy as jnp
from jax import lax
from jax.sharding import PartitionSpec as P


def shifted(value, axis, by):
    size = lax.axis_size(axis)
    pairs = [(i, i + by) for i in range(size) if 0 <= i + by < size]
    return lax.ppermute(value, axis, pairs)


def short_mix(extended, marks, taps, count):
    width = taps.shape[0]
    anchor = marks[width - 1 : width - 1 + count]
    total = jnp.zeros((count, extended.shape[1]), jnp.float32)
    for offset in range(width):
        begin = width - 1 - offset
        same = (marks[begin : begin + count] == anchor).astype(jnp.float32)
        total = (
            total
            + taps[offset].astype(jnp.float32)[None, :]
            * extended[begin : begin + count].astype(jnp.float32)
            * same[:, None]
        )
    return total


def long_mix(extended, marks, filters, bias, count):
    block = filters.shape[0]
    groups = filters.shape[1]
    width = extended.shape[1]
    members = width // groups
    blocks = count // block
    earlier = extended[:count].reshape(blocks, block, width)
    current = extended[block:].reshape(blocks, block, width)
    windows = jnp.concatenate([earlier, current], 1).reshape(blocks, 2 * block, groups, members)
    mark_cols = jnp.concatenate(
        [marks[:count].reshape(blocks, block), marks[block:].reshape(blocks, block)], 1
    )
    mark_rows = marks[block:].reshape(blocks, block)
    row_index = jnp.arange(block)[:, None]
    col_index = jnp.arange(2 * block)[None, :]
    offset = row_index + block - col_index
    valid = (offset >= 0) & (offset < block)
    flipped = jnp.transpose(filters)
    table = flipped[:, jnp.clip(offset, 0, block - 1)]
    table = jnp.where(valid[None], table, jnp.zeros((), jnp.bfloat16))

    def one_block(items):
        window, mark_col, mark_row = items
        same = (mark_col[None, :] == mark_row[:, None]).astype(jnp.bfloat16)
        matrix = table * same[None]
        result = jnp.einsum("gij,jgc->igc", matrix, window, preferred_element_type=jnp.float32)
        return result.reshape(block, width)

    result = lax.map(one_block, (windows, mark_cols, mark_rows)).reshape(count, width)
    return result + bias.astype(jnp.float32)[None, :] * extended[block:].astype(jnp.float32)


def per_device(queries, keys, values, segments, short_filters, mr_filter, mr_bias):
    rows = queries.shape[0]
    width = queries.shape[1]
    block = mr_filter.shape[0]
    reach = short_filters.shape[1]
    lead = block + reach - 1
    edge_marks = shifted(segments[rows - lead :], "tok", 1)
    marks = jnp.concatenate([edge_marks, segments])
    early_q, early_k, early_v = shifted(
        (queries[rows - (reach - 1) :], keys[rows - (lead - 1) :], values[rows - (lead - 1) :]),
        "tok",
        1,
    )
    feat_q = short_mix(jnp.concatenate([early_q, queries]), marks[block:], short_filters[0], rows)
    feat_k = short_mix(
        jnp.concatenate([early_k, keys]), marks[1:], short_filters[1], rows + block - 1
    )
    feat_v = short_mix(
        jnp.concatenate([early_v, values]), marks[1:], short_filters[2], rows + block - 1
    )
    product_wide = (feat_k * feat_v).astype(jnp.bfloat16)
    extended = jnp.concatenate([jnp.zeros((1, width), jnp.bfloat16), product_wide])
    longer = long_mix(extended, marks[reach - 1 :], mr_filter, mr_bias, rows)
    return (feat_q * longer).astype(jnp.bfloat16)


def solution(mesh):
    placed = (
        P(("seq", "tok"), None),
        P(("seq", "tok"), None),
        P(("seq", "tok"), None),
        P(("seq", "tok")),
        P(),
        P(),
        P(),
    )
    return jax.shard_map(
        per_device, mesh=mesh, in_specs=placed, out_specs=P(("seq", "tok"), None), check_vma=False
    )
```

profile of v0, /device:TPU:24, one launch (start us, length us, event | category | flops | bytes accessed | tf_op | source)
XLA Modules:
  0.0 255.6 jit_solution(14970812849470671716)
XLA Ops:
  0.0 0.0 copy-start
  0.0 0.8 slice.134
  0.8 1.9 collective-permute-start.1
  2.7 2.5 slice.140
  5.2 3.5 %collective-permute-start.2 = (bf16[129,4096]{1,0:T(8,128)(2,1)}, bf16[129,4096]{1,0:T(8,128)(2,1)S(1)}, u32[]{:S(2)}, u32[]{:S(2)}) collective-permute-start(bf16[129,4096]{1,0:T(8,128)(2,1)} %slice.140), channel_id=1, source_target_pairs={{0,1},{1,2},{2,3},{3,4},{4,5},{5,6},{6,7},{7,8},{8,9},{9,10},{10,1... | collective-permute-start | bytes 3170312 | tf_op jit(solution)/shard_map/ppermute | solution.py:10
  8.7 2.5 slice.150
  11.3 1.9 collective-permute-start.3
  13.2 0.9 slice.132
  14.0 1.9 collective-permute-start
  16.0 0.1 fusion.14
  16.1 0.1 fusion.17
  16.2 0.1 copy.19
  16.3 0.0 copy-done
  16.3 128.7 %gather_fusion = bf16[32768,256]{1,0:T(8,128)(2,1)} fusion(bf16[256,128]{0,1:T(8,128)(2,1)S(1)} %bitcast.47, s32[32768]{0:T(1024)S(1)} %broadcast_clamp_fusion), kind=kCustom, calls=%fused_computation | custom fusion | bytes 33685504 | tf_op jit(solution)/shard_map/gather | solution.py:47
  145.0 23.2 %copy.14 = bf16[128,256,256]{1,0,2:T(8,128)(2,1)} copy(bf16[128,256,256]{2,1,0:T(8,128)(2,1)} %bitcast.49) | data formatting | bytes 33554432 | tf_op jit(solution)/shard_map/gather | solution.py:47
  168.2 0.0 copy-start.4
  168.2 0.0 copy-start.6
  168.2 0.0 copy-start.5
  168.2 0.0 copy-start.3
  168.2 14.2 %select_bitcast_fusion = bf16[256,128,256]{2,1,0:T(8,128)(2,1)} fusion(bf16[128,256,256]{1,0,2:T(8,128)(2,1)} %copy.14, pred[128,256]{1,0:T(8,128)(4,1)S(1)} %fusion.17), kind=kLoop, calls=%fused_computation.12 | loop fusion | flops 8388608 | bytes 33587200 | tf_op jit(solution)/shard_map/jit(_where)/select_n | solution.py:48
  182.5 0.0 copy-done.4
  182.5 0.1 slice_convert_fusion.8
  182.6 0.0 copy-done.6
  182.6 0.0 collective-permute-done.1
  182.6 0.0 copy-done.5
  182.6 0.1 pad_add_fusion
  182.7 0.1 slice_bitcast_fusion
  182.8 0.1 compare_convert_fusion.2
  182.8 0.1 fusion.18
  182.9 0.0 collective-permute-done.2
  182.9 0.0 collective-permute-done.3
  182.9 0.0 copy-done.3
  182.9 8.8 %multiply_convert_fusion = bf16[383,4096]{1,0:T(8,128)(2,1)S(1)} fusion(bf16[256,4096]{1,0:T(8,128)(2,1)S(1)} %copy-done.3, bf16[256,4096]{1,0:T(8,128)(2,1)} %param.10, bf16[129,4096]{1,0:T(8,128)(2,1)} %collective-permute-done.3, bf16[129,4096]{1,0:T(8,128)(2,1)S(1)} %collective-permute-done.2, f32[4096]{0:T(1024)S(1)} %bitcast.59, f32[4096]{0:T(1024)S(1)} %bitcast.60, ...), kind=kLoop, calls=%fused_computation.13 | loop fusion | flops 62750720 | bytes 9546744 | tf_op jit(solution)/shard_map/convert_element_type | solution.py:81
  191.8 0.0 copy-start.2
  191.8 3.1 %pad_slice_fusion.8 = (bf16[256,4096]{1,0:T(8,128)(2,1)}, bf16[256,4096]{1,0:T(8,128)(2,1)}) fusion(bf16[383,4096]{1,0:T(8,128)(2,1)S(1)} %multiply_convert_fusion), kind=kLoop, calls=%fused_computation.32 | loop fusion | bytes 9437184 | tf_op jit(solution)/shard_map/slice | solution.py:35
  194.9 0.0 copy-done.2
  194.9 3.3 %copy.12 = bf16[256,4096]{0,1:T(8,128)(2,1)S(1)} copy(bf16[256,4096]{1,0:T(8,128)(2,1)} %get-tuple-element.56) | data formatting | bytes 4194304 | tf_op jit(solution)/shard_map/slice | solution.py:35
  198.2 2.1 concatenate.31
  200.2 3.3 %copy.13 = bf16[256,4096]{0,1:T(8,128)(2,1)S(1)} copy(bf16[256,4096]{1,0:T(8,128)(2,1)} %get-tuple-element.57) | data formatting | bytes 4194304 | tf_op jit(solution)/shard_map/slice | solution.py:36
  203.5 2.0 concatenate.32
  205.5 7.9 %pad_maximum_fusion = bf16[2,256,256,16]{1,0,3,2:T(2,128)(2,1)S(1)} fusion(bf16[2,128,256,16]{1,0,3,2:T(2,128)(2,1)} %concatenate.32, bf16[2,128,256,16]{1,0,3,2:T(2,128)(2,1)} %concatenate.31), kind=kLoop, calls=%fused_computation.14 | loop fusion | flops 8388608 | bytes 8388608 | tf_op jit(solution)/shard_map/concatenate | solution.py:37
  213.4 2.7 %copy.15 = bf16[2,256,256,16]{1,3,2,0:T(8,128)(2,1)} copy(bf16[2,256,256,16]{1,0,3,2:T(2,128)(2,1)S(1)} %pad_maximum_fusion) | data formatting | bytes 8388608 | tf_op jit(solution)/shard_map/while | solution.py:57
  216.1 31.9 %while.10 = (s32[]{:T(128)}, f32[2,128,4096]{2,1,0:T(8,128)}, bf16[2,256,256,16]{1,3,2,0:T(8,128)(2,1)}, s32[2,256]{1,0:T(2,128)S(1)}, s32[2,128]{1,0:T(2,128)S(1)}, /*index=5*/bf16[256,128,256]{2,1,0:T(8,128)(2,1)}, s32[]{:T(128)}) while((s32[]{:T(128)}, f32[2,128,4096]{2,1,0:T(8,128)}, bf16[2,256,256,16]{1,3,2,0:T(8,128)(2,1)}, ...), condition=%wide.region_1.2_spmd, body=%wide.region_0.1_spmd.sunk | while | flops 276889600 | bytes 29496916 | solution.py:57
  216.1 0.1 compare_convert_fusion.4
  216.2 10.9 %fusion.27 = f32[256,16,128]{2,1,0:T(8,128)S(1)} fusion(bf16[256,128,256]{2,1,0:T(8,128)(2,1)} %get-tuple-element.127, bf16[128,256]{1,0:T(8,128)(2,1)S(1)} %compare_convert_fusion.4, bf16[2,256,256,16]{1,3,2,0:T(8,128)(2,1)} %get-tuple-element.124, s32[]{:T(128)} %get-tuple-element.115), kind=kOutput, calls=%fused_computation.1.clone.1 | convolution fusion | flops 276824064 | bytes 21037568 | tf_op jit(solution)/shard_map/while/body/eval_jaxpr/gij,jgc->igc/dot_general | solution.py:54
  227.1 1.8 copy.21
  228.9 3.1 %constant_dynamic-update-slice_fusion.2 = f32[2,128,4096]{2,1,0:T(8,128)} fusion(f32[2,128,4096]{2,1,0:T(8,128)} %get-tuple-element.116, f32[1,128,4096]{2,1,0:T(8,128)} %copy.21, s32[]{:T(128)} %get-tuple-element.115), kind=kLoop, calls=%fused_computation.7.clone.1 | loop fusion | bytes 4194816 | tf_op jit(solution)/shard_map/while/body/jit(dynamic_update_index_in_dim)/dynamic_update_slice | solution.py:57
  232.1 0.1 compare_convert_fusion.4
  232.2 10.9 %fusion.27 = f32[256,16,128]{2,1,0:T(8,128)S(1)} fusion(bf16[256,128,256]{2,1,0:T(8,128)(2,1)} %get-tuple-element.127, bf16[128,256]{1,0:T(8,128)(2,1)S(1)} %compare_convert_fusion.4, bf16[2,256,256,16]{1,3,2,0:T(8,128)(2,1)} %get-tuple-element.124, s32[]{:T(128)} %get-tuple-element.115), kind=kOutput, calls=%fused_computation.1.clone.1 | convolution fusion | flops 276824064 | bytes 21037568 | tf_op jit(solution)/shard_map/while/body/eval_jaxpr/gij,jgc->igc/dot_general | solution.py:54
  243.0 1.8 copy.21
  244.9 3.1 %constant_dynamic-update-slice_fusion.2 = f32[2,128,4096]{2,1,0:T(8,128)} fusion(f32[2,128,4096]{2,1,0:T(8,128)} %get-tuple-element.116, f32[1,128,4096]{2,1,0:T(8,128)} %copy.21, s32[]{:T(128)} %get-tuple-element.115), kind=kLoop, calls=%fused_computation.7.clone.1 | loop fusion | bytes 4194816 | tf_op jit(solution)/shard_map/while/body/jit(dynamic_update_index_in_dim)/dynamic_update_slice | solution.py:57
  248.0 0.0 collective-permute-done
  248.0 0.0 copy-start.1
  248.0 7.6 %fusion.8 = bf16[256,4096]{1,0:T(8,128)(2,1)} fusion(f32[2,128,4096]{2,1,0:T(8,128)} %get-tuple-element.37, bf16[256,4096]{1,0:T(8,128)(2,1)} %param.9, bf16[2,4096]{1,0:T(2,128)(2,1)S(1)} %collective-permute-done, f32[4096]{0:T(1024)S(1)} %convert_element_type.189, f32[256]{0:T(256)S(1)} %get-tuple-element.68, f32[4096]{0:T(1024)S(1)} %bitcast.53, ...), kind=kLoop, calls=%fused_computation.17 | loop fusion | flops 22020096 | bytes 10569728 | tf_op jit(solution)/shard_map/convert_element_type | solution.py:84
  255.6 0.0 copy-done.1
  (9 shorter events, 0.1 us)
Async XLA Ops:
  0.0 16.3 %copy-start = (bf16[128,256]{1,0:T(8,128)(2,1)S(1)}, bf16[128,256]{1,0:T(8,128)(2,1)}, u32[]{:S(2)}) copy-start(bf16[128,256]{1,0:T(8,128)(2,1)} %param.14) | copy-start | bytes 196612
  0.8 181.8 %collective-permute-start.1 = (s32[130]{0:T(256)S(1)}, s32[130]{0:T(256)S(1)}, u32[]{:S(2)}, u32[]{:S(2)}) collective-permute-start(s32[130]{0:T(256)S(1)} %slice.134), channel_id=1, source_target_pairs={{0,1},{1,2},{2,3},{3,4},{4,5},{5,6},{6,7},{7,8},{8,9},{9,10},{10,1... | collective-permute-start | bytes 1568 | tf_op jit(solution)/shard_map/ppermute | solution.py:10
  5.2 177.7 %collective-permute-start.2 = (bf16[129,4096]{1,0:T(8,128)(2,1)}, bf16[129,4096]{1,0:T(8,128)(2,1)S(1)}, u32[]{:S(2)}, u32[]{:S(2)}) collective-permute-start(bf16[129,4096]{1,0:T(8,128)(2,1)} %slice.140), channel_id=1, source_target_pairs={{0,1},{1,2},{2,3},{3,4},{4,5},{5,6},{6,7},{7,8},{8,9},{9,10},{10,1... | collective-permute-start | bytes 3170312 | tf_op jit(solution)/shard_map/ppermute | solution.py:10
  11.3 171.7 %collective-permute-start.3 = (bf16[129,4096]{1,0:T(8,128)(2,1)}, bf16[129,4096]{1,0:T(8,128)(2,1)}, u32[]{:S(2)}, u32[]{:S(2)}) collective-permute-start(bf16[129,4096]{1,0:T(8,128)(2,1)} %slice.150), channel_id=1, source_target_pairs={{0,1},{1,2},{2,3},{3,4},{4,5},{5,6},{6,7},{7,8},{8,9},{9,10},{10,1... | collective-permute-start | bytes 3170312 | tf_op jit(solution)/shard_map/ppermute | solution.py:10
  14.0 234.0 %collective-permute-start = (bf16[2,4096]{1,0:T(2,128)(2,1)S(1)}, bf16[2,4096]{1,0:T(2,128)(2,1)S(1)}, u32[]{:S(2)}, u32[]{:S(2)}) collective-permute-start(bf16[2,4096]{1,0:T(2,128)(2,1)S(1)} %slice.132), channel_id=1, source_target_pairs={{0,1},{1,2},{2,3},{3,4},{4,5},{5,6},{6,7},{7,8},{8,9},{9,10},{10,1... | collective-permute-start | bytes 49160 | tf_op jit(solution)/shard_map/ppermute | solution.py:10
  168.2 14.3 %copy-start.4 = (bf16[3,3,4096]{2,1,0:T(4,128)(2,1)S(1)}, bf16[3,3,4096]{2,1,0:T(4,128)(2,1)}, u32[]{:S(2)}) copy-start(bf16[3,3,4096]{2,1,0:T(4,128)(2,1)} %param.13) | copy-start | bytes 221188
  168.2 14.4 %copy-start.6 = (bf16[4096]{0:T(1024)(128)(2,1)S(1)}, bf16[4096]{0:T(1024)(128)(2,1)}, u32[]{:S(2)}) copy-start(bf16[4096]{0:T(1024)(128)(2,1)} %param.15) | copy-start | bytes 24580
  168.2 14.4 %copy-start.5 = (s32[256]{0:T(256)S(1)}, s32[256]{0:T(256)}, u32[]{:S(2)}) copy-start(s32[256]{0:T(256)} %param.12) | copy-start | bytes 3076
  168.2 14.7 %copy-start.3 = (bf16[256,4096]{1,0:T(8,128)(2,1)S(1)}, bf16[256,4096]{1,0:T(8,128)(2,1)}, u32[]{:S(2)}) copy-start(bf16[256,4096]{1,0:T(8,128)(2,1)} %param.11) | copy-start | bytes 6291460
  191.8 3.1 %copy-start.2 = (bf16[383,4096]{1,0:T(8,128)(2,1)}, bf16[383,4096]{1,0:T(8,128)(2,1)S(1)}, u32[]{:S(2)}) copy-start(bf16[383,4096]{1,0:T(8,128)(2,1)S(1)} %multiply_convert_fusion) | copy-start | bytes 9412612
  248.0 7.6 %copy-start.1 = (bf16[128,256]{1,0:T(8,128)(2,1)S(1)}, bf16[128,256]{1,0:T(8,128)(2,1)}, u32[]{:S(2)}) copy-start(bf16[128,256]{1,0:T(8,128)(2,1)} %param.14) | copy-start | bytes 196612
where the time goes:
time: 260 us; the launch traced here: 256 us
  local copies, waits for them, and re-layouts  185 us (71%)
  other arithmetic  39.3 us (15%)
  matrix products  21.8 us (8%)
  starting transfers between devices  9.26 us (4%)
    gather x2, local copies, waits for them, and re-layouts, long_mix(): table = flipped[:, jnp.clip(offset, 0, block - 1)]  152 us
    dot_general x2, matrix products, one_block(): jnp.einsum('gij,jgc->igc', matrix, window, preferred_element_type=jnp.flo...  21.8 us
    select_n x1, other arithmetic, long_mix(): table = jnp.where(valid[None], table, jnp.zeros((), jnp.bfloat16))  14.2 us
    dynamic_update_slice x4, local copies, waits for them, and re-layouts, long_mix(): lax.map(one_block, (windows, mark_cols, mark_rows)).reshape(count, width)  9.91 us
    ppermute x4, starting transfers between devices, shifted(): return lax.ppermute(value, axis, pairs)  9.26 us
    convert_element_type x1, other arithmetic, per_device(): product_wide = (feat_k * feat_v).astype(jnp.bfloat16)  8.82 us
    concatenate x1, other arithmetic, long_mix(): jnp.concatenate([earlier, current], 1)  7.88 us
    convert_element_type x1, other arithmetic, per_device(): return (feat_q * longer).astype(jnp.bfloat16)  7.59 us
  transfers between devices with their start and end apart: 4, of which 0 were waited for; matrix products, arithmetic and copies ran while one was open for 93% of the time, Pallas kernels for 0%

commit v1 on v0

v1 whole, which is shorter than its diff:
```python
import functools

import jax
import jax.numpy as jnp
from jax import lax
from jax.experimental import pallas as pl
from jax.experimental.pallas import tpu as pltpu
from jax.sharding import PartitionSpec as P

LANES = 128
TILE = 512
CHUNKS = 4


def shifted(value, axis, by):
    size = lax.axis_size(axis)
    pairs = [(i, i + by) for i in range(size) if 0 <= i + by < size]
    return lax.ppermute(value, axis, pairs)


def column(row, block):
    return jnp.transpose(jnp.broadcast_to(row, (block, block)))


def feature(x, before, taps, one, two):
    x = x.astype(jnp.float32)
    before = before.astype(jnp.float32)
    taps = taps.astype(jnp.float32)
    at = lax.broadcasted_iota(jnp.int32, x.shape, 0)
    far, near = before[0:1], before[1:2]
    x1 = jnp.where(at == 0, near, pltpu.roll(x, 1, 0))
    x2 = jnp.where(at == 0, far, jnp.where(at == 1, near, pltpu.roll(x, 2, 0)))
    return taps[0:1] * x + (taps[1:2] * x1) * one + (taps[2:3] * x2) * two


def short_marks(info, start, block):
    return (
        column(info[1:2, start : start + block], block),
        column(info[2:3, start : start + block], block),
    )


def tail_kernel(k, v, ke, ve, taps, info, out, one_ref, two_ref):
    block = k.shape[0]

    @pl.when(pl.program_id(0) == 0)
    def _():
        one_ref[...], two_ref[...] = short_marks(info, 2 * block, block)

    one, two = one_ref[...], two_ref[...]
    for s in range(0, k.shape[1], LANES):
        at = slice(s, s + LANES)
        fk = feature(k[:, at], ke[14:16, at], taps[1, :, at], one, two)
        fv = feature(v[:, at], ve[14:16, at], taps[2, :, at], one, two)
        out[:, at] = (fk * fv).astype(out.dtype)


def prepare(info, filters, hrev, upper, lower, start, block):
    tap = lax.broadcasted_iota(jnp.int32, (block, block), 0)
    lane = lax.broadcasted_iota(jnp.int32, (block, block), 1)
    turn = (tap == lax.rem(block - lane, block)).astype(jnp.bfloat16)
    hrev[...] = lax.dot_general(
        filters[...], turn, (((0,), (0,)), ((), ())), preferred_element_type=jnp.float32
    )
    own = column(info[0:1, start : start + block], block)
    prev_row = info[0:1, start - block : start]
    own_row = info[0:1, start : start + block]
    upper[...] = jnp.where((own == prev_row) & (lane > tap), 1.0, 0.0).astype(jnp.bfloat16)
    lower[...] = jnp.where((own == own_row) & (lane <= tap), 1.0, 0.0).astype(jnp.bfloat16)


def long_tile(prev, cur, hrev, first, members, upper, lower):
    block = prev.shape[0]
    window = jnp.concatenate([prev, cur], 0)
    lane = lax.broadcasted_iota(jnp.int32, (block, LANES), 1)
    total = None
    for g in range(LANES // members):
        base = jnp.broadcast_to(hrev[pl.ds(first + g, 1), :], (block, block))
        ring = pltpu.roll(base, 0, 1, stride=1, stride_axis=0).astype(jnp.bfloat16)
        table = jnp.concatenate([ring * upper, ring * lower], 1)
        part = jnp.dot(table, window, preferred_element_type=jnp.float32)
        total = part if g == 0 else jnp.where(lane < g * members, total, part)
    return total


def back_kernel(members, q, qe, k, v, edge, ptail, taps, bias, info, filters,
                out, phead, hrev, upper, lower, one_ref, two_ref, hone_ref, htwo_ref):
    block = q.shape[0]
    step = pl.program_id(0)

    @pl.when(step == 0)
    def _():
        prepare(info, filters, hrev, upper, lower, 2 * block, block)
        one_ref[...], two_ref[...] = short_marks(info, 2 * block, block)
        hone_ref[...], htwo_ref[...] = short_marks(info, block, block)

    up, low = upper[...], lower[...]
    per = LANES // members
    for s in range(0, q.shape[1], LANES):
        at = slice(s, s + LANES)
        hone, htwo = hone_ref[...], htwo_ref[...]
        fk = feature(k[:, at], edge[2:4, at], taps[1, :, at], hone, htwo)
        fv = feature(v[:, at], edge[4:6, at], taps[2, :, at], hone, htwo)
        prev = (fk * fv).astype(jnp.bfloat16)
        phead[:, at] = prev
        cur = ptail[:, at]
        first = step * (q.shape[1] // members) + (s // LANES) * per
        longer = long_tile(prev, cur, hrev, first, members, up, low)
        longer = longer + bias[:, at].astype(jnp.float32) * cur.astype(jnp.float32)
        fq = feature(q[:, at], qe[14:16, at], taps[0, :, at], one_ref[...], two_ref[...])
        out[:, at] = (fq * longer).astype(out.dtype)


def front_kernel(members, base, q, edge, halo, phead, taps, bias, info, filters, whole,
                 out, hrev, upper, lower, one_ref, two_ref):
    del whole
    block = q.shape[0]
    step = pl.program_id(0)

    @pl.when(step == 0)
    def _():
        prepare(info, filters, hrev, upper, lower, block, block)
        one_ref[...], two_ref[...] = short_marks(info, block, block)

    up, low = upper[...], lower[...]
    per = LANES // members
    for s in range(0, q.shape[1], LANES):
        at = slice(s, s + LANES)
        cur = phead[:, at]
        first = (base + step) * (q.shape[1] // members) + (s // LANES) * per
        longer = long_tile(halo[:, at], cur, hrev, first, members, up, low)
        longer = longer + bias[:, at].astype(jnp.float32) * cur.astype(jnp.float32)
        fq = feature(q[:, at], edge[0:2, at], taps[0, :, at], one_ref[...], two_ref[...])
        out[:, at] = (fq * longer).astype(out.dtype)


def marks_of(segments_ext):
    seg = segments_ext.astype(jnp.float32)
    one = jnp.concatenate([jnp.zeros((1,), jnp.float32), (seg[1:] == seg[:-1]).astype(jnp.float32)])
    two = jnp.concatenate([jnp.zeros((2,), jnp.float32), (seg[2:] == seg[:-2]).astype(jnp.float32)])
    return jnp.stack([seg, one, two])


def per_device(queries, keys, values, segments, short_filters, mr_filter, mr_bias):
    rows, width = queries.shape
    block, groups = mr_filter.shape
    members = width // groups
    reach = short_filters.shape[1]
    tile = min(TILE, width // CHUNKS)
    sub = block // 16
    bf16, f32 = jnp.bfloat16, jnp.float32
    bias = mr_bias.reshape(1, width)
    edge = jnp.concatenate([x[rows - (reach - 1):] for x in (queries, keys, values)])
    edge = shifted(edge, "tok", 1)
    edge_marks = shifted(segments[rows - block:], "tok", 1)
    info_own = marks_of(jnp.concatenate([jnp.zeros((block,), jnp.int32), segments]))
    info = marks_of(jnp.concatenate([edge_marks, segments]))

    full = lambda a: pl.BlockSpec(a.shape, lambda c: (0,) * a.ndim)
    blk = lambda r: pl.BlockSpec((block, tile), lambda c: (r, c))
    last = pl.BlockSpec((16, tile), lambda c: (sub - 1, c))
    tap_spec = pl.BlockSpec((3, reach, tile), lambda c: (0, 0, c))
    square = lambda t: pltpu.VMEM((block, block), t)
    row = pl.BlockSpec((1, tile), lambda c: (0, c))
    edge_spec = pl.BlockSpec((edge.shape[0], tile), lambda c: (0, c))
    half_shape = jax.ShapeDtypeStruct((block, width), bf16)

    ptail = pl.pallas_call(
        tail_kernel,
        grid=(width // tile,),
        in_specs=[blk(1), blk(1), last, last, tap_spec, full(info_own)],
        out_specs=blk(0),
        out_shape=half_shape,
        scratch_shapes=[square(f32), square(f32)],
        cost_estimate=pl.CostEstimate(flops=10**7, bytes_accessed=3 * 2**20, transcendentals=0),
    )(keys, values, keys, values, short_filters, info_own)

    cut = width // CHUNKS
    halos = [shifted(ptail[:, i * cut : (i + 1) * cut], "tok", 1) for i in range(CHUNKS)]

    out, phead = pl.pallas_call(
        functools.partial(back_kernel, members),
        grid=(width // tile,),
        in_specs=[blk(1), last, blk(0), blk(0), edge_spec, blk(0), tap_spec, row,
                  full(info), full(mr_filter)],
        out_specs=[blk(1), blk(0)],
        out_shape=[jax.ShapeDtypeStruct((rows, width), bf16), half_shape],
        scratch_shapes=[pltpu.VMEM((groups, block), f32), square(bf16), square(bf16)]
        + [square(f32)] * 4,
        cost_estimate=pl.CostEstimate(flops=10**10, bytes_accessed=6 * 2**20, transcendentals=0),
    )(queries, queries, keys, values, edge, ptail, short_filters, bias, info, mr_filter)

    for i in range(CHUNKS):
        base = i * (cut // tile)
        off = lambda shape, z, base=base: pl.BlockSpec(shape, lambda c: z + (base + c,))
        out = pl.pallas_call(
            functools.partial(front_kernel, members, base),
            grid=(cut // tile,),
            in_specs=[
                off((block, tile), (0,)),
                off((edge.shape[0], tile), (0,)),
                pl.BlockSpec((block, tile), lambda c: (0, c)),
                off((block, tile), (0,)),
                off((3, reach, tile), (0, 0)),
                off((1, tile), (0,)),
                full(info),
                full(mr_filter),
                pl.BlockSpec(memory_space=pl.ANY),
            ],
            out_specs=off((block, tile), (0,)),
            out_shape=jax.ShapeDtypeStruct((rows, width), bf16),
            input_output_aliases={8: 0},
            scratch_shapes=[pltpu.VMEM((groups, block), f32), square(bf16), square(bf16)]
            + [square(f32)] * 2,
            cost_estimate=pl.CostEstimate(
                flops=10**10 // CHUNKS, bytes_accessed=4 * 2**20 // CHUNKS, transcendentals=0
            ),
        )(queries, edge, halos[i], phead, short_filters, bias, info, mr_filter, out)
    return out


def solution(mesh):
    placed = (
        P(("seq", "tok"), None),
        P(("seq", "tok"), None),
        P(("seq", "tok"), None),
        P(("seq", "tok")),
        P(),
        P(),
        P(),
    )
    return jax.shard_map(
        per_device, mesh=mesh, in_specs=placed, out_specs=P(("seq", "tok"), None), check_vma=False
    )
```

time: 260 us -> 62.1 us (0.24)
  the two profiles are of different devices: /device:TPU:24 before, /device:TPU:0 now
where the time goes in v1:
time: 62.1 us; the launch traced here: 61.2 us
  Pallas kernels  31.5 us (51%)
  starting transfers between devices  17.8 us (29%)
  local copies, waits for them, and re-layouts  9.36 us (15%)
  other arithmetic  2.41 us (4%)
    ppermute x6, starting transfers between devices, shifted(): return lax.ppermute(value, axis, pairs)  17.8 us
    pallas_call x4, Pallas kernels, per_device(): pl.pallas_call(functools.partial(front_kernel, members, base), grid=(cut...  14.6 us
    pallas_call x1, Pallas kernels, per_device(): pl.pallas_call(functools.partial(back_kernel, members), grid=(width // ti...  10.3 us
    pallas_call x1, Pallas kernels, per_device(): pl.pallas_call(tail_kernel, grid=(width // tile,), in_specs=[blk(1), blk(...  6.61 us
    unnamed x12, local copies, waits for them, and re-layouts  3.49 us
    slice x3, local copies, waits for them, and re-layouts, per_device(): x[rows - (reach - 1):]  2.59 us
    another operation x6, other arithmetic, marks_of(): return jnp.stack([seg, one, two])  1.5 us
    reshape x1, local copies, waits for them, and re-layouts, per_device(): bias = mr_bias.reshape(1, width)  1.3 us
  transfers between devices with their start and end apart: 6, of which 0 were waited for; matrix products, arithmetic and copies ran while one was open for 12% of the time, Pallas kernels for 45%

profile of v1, /device:TPU:0, one launch (start us, length us, event | category | flops | bytes accessed | tf_op | source)
XLA Modules:
  0.0 61.2 jit_solution(4618329577088336192)
XLA Ops:
  0.0 0.7 %slice.56 = s32[128]{0:T(128)S(1)} slice(s32[256]{0:T(256)} %param.10), slice={[128:256]} | slice | bytes 1024 | tf_op jit(solution)/shard_map/slice | solution.py:155
  0.7 2.4 %collective-permute-start.2 = (s32[128]{0:T(128)S(1)}, s32[128]{0:T(128)S(1)}, u32[]{:S(2)}, u32[]{:S(2)}) collective-permute-start(s32[128]{0:T(128)S(1)} %slice.56), channel_id=1, source_target_pairs={{0,1},{1,2},{2,3},{3,4},{4,5},{5,6},{6,7},{7,8},{8,9},{9,10},{10,1... | collective-permute-start | bytes 1544 | tf_op jit(solution)/shard_map/ppermute | solution.py:18
  3.1 0.9 %slice.49 = bf16[2,4096]{1,0:T(2,128)(2,1)S(1)} slice(bf16[256,4096]{1,0:T(8,128)(2,1)} %k.3), slice={[254:256], [0:4096]} | slice | bytes 32768 | tf_op jit(solution)/shard_map/slice | solution.py:153
  3.9 0.9 %slice.50 = bf16[2,4096]{1,0:T(2,128)(2,1)S(1)} slice(bf16[256,4096]{1,0:T(8,128)(2,1)} %v.3), slice={[254:256], [0:4096]} | slice | bytes 32768 | tf_op jit(solution)/shard_map/slice | solution.py:153
  4.8 0.9 %slice.48 = bf16[2,4096]{1,0:T(2,128)(2,1)S(1)} slice(bf16[256,4096]{1,0:T(8,128)(2,1)} %q.9), slice={[254:256], [0:4096]} | slice | bytes 32768 | tf_op jit(solution)/shard_map/slice | solution.py:153
  5.7 0.1 pad_maximum_fusion
  5.7 4.5 %collective-permute-start = (bf16[6,4096]{1,0:T(8,128)(2,1)S(1)}, bf16[6,4096]{1,0:T(8,128)(2,1)S(1)}, u32[]{:S(2)}, u32[]{:S(2)}) collective-permute-start(bf16[6,4096]{1,0:T(8,128)(2,1)S(1)} %pad_maximum_fusion), channel_id=1, source_target_pairs={{0,1},{1,2},{2,3},{3,4},{4,5},{5,6},{6,7},{7,8},{8,9},{9,10},{10,1... | collective-permute-start | bytes 147464 | tf_op jit(solution)/shard_map/ppermute | solution.py:18
  10.3 1.3 %reshape.32.bias = bf16[1,4096]{1,0:T(2,128)(2,1)} reshape(bf16[4096]{0:T(1024)(128)(2,1)} %param.13) | data formatting | bytes 16384 | tf_op jit(solution)/shard_map/reshape | solution.py:152
  11.6 0.0 collective-permute-done.2
  11.6 0.7 %fusion = (f32[384]{0:T(512)S(1)}, f32[384]{0:T(512)S(1)}) fusion(s32[256]{0:T(256)} %param.10, s32[128]{0:T(128)S(1)} %collective-permute-done.2), kind=kLoop, calls=%fused_computation.7 | loop fusion | flops 1152 | bytes 4608 | tf_op jit(solution)/shard_map/convert_element_type | solution.py:138
  12.3 0.1 slice_compare_fusion.1
  12.3 0.1 slice_compare_fusion
  12.4 0.1 fusion.2
  12.5 0.1 fusion.1
  12.6 0.1 pad_convert_fusion.1
  12.7 0.1 pad_convert_fusion.2
  12.8 0.6 pad_maximum_fusion.1.info
  13.4 6.6 %shard_map.73.ptail = bf16[128,4096]{1,0:T(8,128)(2,1)} custom-call(bf16[256,4096]{1,0:T(8,128)(2,1)} %k.3, bf16[256,4096]{1,0:T(8,128)(2,1)} %v.3, bf16[256,4096]{1,0:T(8,128)(2,1)} %k.3, bf16[256,4096]{1,0:T(8,128)(2,1)} %v.3, bf16[3,3,4096]{2,1,0:T(4,128)(2,1)} %taps.11, f32[3,384]{1,0:T(4,128)} %pad_maximum_fusion.1.info), custom_call_target="tpu_custom_call" | custom-call | flops 10000000 | bytes 3145728 | tf_op jit(solution)/shard_map/pallas_call | solution.py:168
  20.0 0.0 copy-start
  20.0 1.3 %fusion.3 = (bf16[128,1024]{1,0:T(8,128)(2,1)S(1)}, bf16[128,1024]{1,0:T(8,128)(2,1)S(1)}, bf16[128,1024]{1,0:T(8,128)(2,1)S(1)}, bf16[128,1024]{1,0:T(8,128)(2,1)S(1)}) fusion(bf16[128,4096]{1,0:T(8,128)(2,1)} %shard_map.73.ptail), kind=kLoop, calls=%fused_computation.17 | loop fusion | bytes 2097152 | tf_op jit(solution)/shard_map/slice | solution.py:179
  21.2 1.9 %collective-permute-start.5 = (bf16[128,1024]{1,0:T(8,128)(2,1)S(1)}, bf16[128,1024]{1,0:T(8,128)(2,1)S(1)}, u32[]{:S(2)}, u32[]{:S(2)}) collective-permute-start(bf16[128,1024]{1,0:T(8,128)(2,1)S(1)} %get-tuple-element.9), channel_id=1, source_target_pairs={{0,1},{1,2},{2,3},{3,4},{4,5},{5,6},{6,7},{7,8},{8,9},{9,10},{10,1... | collective-permute-start | bytes 786440 | tf_op jit(solution)/shard_map/ppermute | solution.py:18
  23.2 3.5 %collective-permute-start.4 = (bf16[128,1024]{1,0:T(8,128)(2,1)S(1)}, bf16[128,1024]{1,0:T(8,128)(2,1)S(1)}, u32[]{:S(2)}, u32[]{:S(2)}) collective-permute-start(bf16[128,1024]{1,0:T(8,128)(2,1)S(1)} %get-tuple-element.10), channel_id=1, source_target_pairs={{0,1},{1,2},{2,3},{3,4},{4,5},{5,6},{6,7},{7,8},{8,9},{9,10},{10,1... | collective-permute-start | bytes 786440 | tf_op jit(solution)/shard_map/ppermute | solution.py:18
  26.7 1.9 %collective-permute-start.3 = (bf16[128,1024]{1,0:T(8,128)(2,1)S(1)}, bf16[128,1024]{1,0:T(8,128)(2,1)S(1)}, u32[]{:S(2)}, u32[]{:S(2)}) collective-permute-start(bf16[128,1024]{1,0:T(8,128)(2,1)S(1)} %get-tuple-element.11), channel_id=1, source_target_pairs={{0,1},{1,2},{2,3},{3,4},{4,5},{5,6},{6,7},{7,8},{8,9},{9,10},{10,1... | collective-permute-start | bytes 786440 | tf_op jit(solution)/shard_map/ppermute | solution.py:18
  28.7 3.5 %collective-permute-start.1 = (bf16[128,1024]{1,0:T(8,128)(2,1)S(1)}, bf16[128,1024]{1,0:T(8,128)(2,1)S(1)}, u32[]{:S(2)}, u32[]{:S(2)}) collective-permute-start(bf16[128,1024]{1,0:T(8,128)(2,1)S(1)} %get-tuple-element.12), channel_id=1, source_target_pairs={{0,1},{1,2},{2,3},{3,4},{4,5},{5,6},{6,7},{7,8},{8,9},{9,10},{10,1... | collective-permute-start | bytes 786440 | tf_op jit(solution)/shard_map/ppermute | solution.py:18
  32.2 0.0 copy-done
  32.2 0.6 pad_maximum_fusion.2.info
  32.8 0.0 collective-permute-done.edge
  32.8 0.0 copy-start.5
  32.8 0.6 copy-done.5
  33.4 10.3 %shard_map.74 = (bf16[256,4096]{1,0:T(8,128)(2,1)}, bf16[128,4096]{1,0:T(8,128)(2,1)}) custom-call(bf16[256,4096]{1,0:T(8,128)(2,1)} %q.9, bf16[256,4096]{1,0:T(8,128)(2,1)} %q.9, bf16[256,4096]{1,0:T(8,128)(2,1)} %k.3, bf16[256,4096]{1,0:T(8,128)(2,1)} %v.3, bf16[6,4096]{1,0:T(8,128)(2,1)} %copy-done.5, bf16[128,4096]{1,0:T(8,128)(2,1)} %shard_map.73.ptail, ...), custom_call_target="tpu_custom_call" | custom-call | flops 10000000000 | bytes 6291456 | tf_op jit(solution)/shard_map/pallas_call | solution.py:181
  43.7 0.0 collective-permute-done.5.halo
  43.7 0.0 copy-start.4
  43.8 0.7 %copy-done.4 = bf16[128,1024]{1,0:T(8,128)(2,1)} copy-done((bf16[128,1024]{1,0:T(8,128)(2,1)}, bf16[128,1024]{1,0:T(8,128)(2,1)S(1)}, u32[]{:S(2)}) %copy-start.4) | copy-done | bytes 262168
  44.5 3.6 %shard_map.75.whole = bf16[256,4096]{1,0:T(8,128)(2,1)} custom-call(bf16[256,4096]{1,0:T(8,128)(2,1)} %q.9, bf16[6,4096]{1,0:T(8,128)(2,1)} %copy-done.5, bf16[128,1024]{1,0:T(8,128)(2,1)} %copy-done.4, bf16[128,4096]{1,0:T(8,128)(2,1)} %get-tuple-element.7.phead, bf16[3,3,4096]{2,1,0:T(4,128)(2,1)} %taps.11, ...), custom_call_target="tpu_custom_call", output_to_operand_aliasing={{}: (8, {})} | custom-call | flops 2500000000 | bytes 1048576 | tf_op jit(solution)/shard_map/pallas_call | solution.py:196
  48.1 0.0 collective-permute-done.4.halo
  48.1 0.0 copy-start.3
  48.1 0.7 %copy-done.3 = bf16[128,1024]{1,0:T(8,128)(2,1)} copy-done((bf16[128,1024]{1,0:T(8,128)(2,1)}, bf16[128,1024]{1,0:T(8,128)(2,1)S(1)}, u32[]{:S(2)}) %copy-start.3) | copy-done | bytes 262168
  48.8 3.6 %shard_map.76.whole = bf16[256,4096]{1,0:T(8,128)(2,1)} custom-call(bf16[256,4096]{1,0:T(8,128)(2,1)} %q.9, bf16[6,4096]{1,0:T(8,128)(2,1)} %copy-done.5, bf16[128,1024]{1,0:T(8,128)(2,1)} %copy-done.3, bf16[128,4096]{1,0:T(8,128)(2,1)} %get-tuple-element.7.phead, bf16[3,3,4096]{2,1,0:T(4,128)(2,1)} %taps.11, ...), custom_call_target="tpu_custom_call", output_to_operand_aliasing={{}: (8, {})} | custom-call | flops 2500000000 | bytes 1048576 | tf_op jit(solution)/shard_map/pallas_call | solution.py:196
  52.5 0.0 collective-permute-done.3.halo
  52.5 0.0 copy-start.2
  52.5 0.7 %copy-done.2 = bf16[128,1024]{1,0:T(8,128)(2,1)} copy-done((bf16[128,1024]{1,0:T(8,128)(2,1)}, bf16[128,1024]{1,0:T(8,128)(2,1)S(1)}, u32[]{:S(2)}) %copy-start.2) | copy-done | bytes 262168
  53.2 3.6 %shard_map.77.whole = bf16[256,4096]{1,0:T(8,128)(2,1)} custom-call(bf16[256,4096]{1,0:T(8,128)(2,1)} %q.9, bf16[6,4096]{1,0:T(8,128)(2,1)} %copy-done.5, bf16[128,1024]{1,0:T(8,128)(2,1)} %copy-done.2, bf16[128,4096]{1,0:T(8,128)(2,1)} %get-tuple-element.7.phead, bf16[3,3,4096]{2,1,0:T(4,128)(2,1)} %taps.11, ...), custom_call_target="tpu_custom_call", output_to_operand_aliasing={{}: (8, {})} | custom-call | flops 2500000000 | bytes 1048576 | tf_op jit(solution)/shard_map/pallas_call | solution.py:196
  56.9 0.0 collective-permute-done.1.halo
  56.9 0.0 copy-start.1
  56.9 0.7 %copy-done.1 = bf16[128,1024]{1,0:T(8,128)(2,1)} copy-done((bf16[128,1024]{1,0:T(8,128)(2,1)}, bf16[128,1024]{1,0:T(8,128)(2,1)S(1)}, u32[]{:S(2)}) %copy-start.1) | copy-done | bytes 262168
  57.6 3.6 %shard_map.78 = bf16[256,4096]{1,0:T(8,128)(2,1)} custom-call(bf16[256,4096]{1,0:T(8,128)(2,1)} %q.9, bf16[6,4096]{1,0:T(8,128)(2,1)} %copy-done.5, bf16[128,1024]{1,0:T(8,128)(2,1)} %copy-done.1, bf16[128,4096]{1,0:T(8,128)(2,1)} %get-tuple-element.7.phead, bf16[3,3,4096]{2,1,0:T(4,128)(2,1)} %taps.11, ...), custom_call_target="tpu_custom_call", output_to_operand_aliasing={{}: (8, {})} | custom-call | flops 2500000000 | bytes 1048576 | tf_op jit(solution)/shard_map/pallas_call | solution.py:196
  (6 shorter events, 0.0 us)
Async XLA Ops:
  0.7 10.9 %collective-permute-start.2 = (s32[128]{0:T(128)S(1)}, s32[128]{0:T(128)S(1)}, u32[]{:S(2)}, u32[]{:S(2)}) collective-permute-start(s32[128]{0:T(128)S(1)} %slice.56), channel_id=1, source_target_pairs={{0,1},{1,2},{2,3},{3,4},{4,5},{5,6},{6,7},{7,8},{8,9},{9,10},{10,1... | collective-permute-start | bytes 1544 | tf_op jit(solution)/shard_map/ppermute | solution.py:18
  5.7 27.1 %collective-permute-start = (bf16[6,4096]{1,0:T(8,128)(2,1)S(1)}, bf16[6,4096]{1,0:T(8,128)(2,1)S(1)}, u32[]{:S(2)}, u32[]{:S(2)}) collective-permute-start(bf16[6,4096]{1,0:T(8,128)(2,1)S(1)} %pad_maximum_fusion), channel_id=1, source_target_pairs={{0,1},{1,2},{2,3},{3,4},{4,5},{5,6},{6,7},{7,8},{8,9},{9,10},{10,1... | collective-permute-start | bytes 147464 | tf_op jit(solution)/shard_map/ppermute | solution.py:18
  20.0 12.2 %copy-start = (s32[256]{0:T(256)S(1)}, s32[256]{0:T(256)}, u32[]{:S(2)}) copy-start(s32[256]{0:T(256)} %param.10) | copy-start | bytes 3076
  21.2 22.5 %collective-permute-start.5 = (bf16[128,1024]{1,0:T(8,128)(2,1)S(1)}, bf16[128,1024]{1,0:T(8,128)(2,1)S(1)}, u32[]{:S(2)}, u32[]{:S(2)}) collective-permute-start(bf16[128,1024]{1,0:T(8,128)(2,1)S(1)} %get-tuple-element.9), channel_id=1, source_target_pairs={{0,1},{1,2},{2,3},{3,4},{4,5},{5,6},{6,7},{7,8},{8,9},{9,10},{10,1... | collective-permute-start | bytes 786440 | tf_op jit(solution)/shard_map/ppermute | solution.py:18
  23.2 24.9 %collective-permute-start.4 = (bf16[128,1024]{1,0:T(8,128)(2,1)S(1)}, bf16[128,1024]{1,0:T(8,128)(2,1)S(1)}, u32[]{:S(2)}, u32[]{:S(2)}) collective-permute-start(bf16[128,1024]{1,0:T(8,128)(2,1)S(1)} %get-tuple-element.10), channel_id=1, source_target_pairs={{0,1},{1,2},{2,3},{3,4},{4,5},{5,6},{6,7},{7,8},{8,9},{9,10},{10,1... | collective-permute-start | bytes 786440 | tf_op jit(solution)/shard_map/ppermute | solution.py:18
  26.7 25.8 %collective-permute-start.3 = (bf16[128,1024]{1,0:T(8,128)(2,1)S(1)}, bf16[128,1024]{1,0:T(8,128)(2,1)S(1)}, u32[]{:S(2)}, u32[]{:S(2)}) collective-permute-start(bf16[128,1024]{1,0:T(8,128)(2,1)S(1)} %get-tuple-element.11), channel_id=1, source_target_pairs={{0,1},{1,2},{2,3},{3,4},{4,5},{5,6},{6,7},{7,8},{8,9},{9,10},{10,1... | collective-permute-start | bytes 786440 | tf_op jit(solution)/shard_map/ppermute | solution.py:18
  28.7 28.2 %collective-permute-start.1 = (bf16[128,1024]{1,0:T(8,128)(2,1)S(1)}, bf16[128,1024]{1,0:T(8,128)(2,1)S(1)}, u32[]{:S(2)}, u32[]{:S(2)}) collective-permute-start(bf16[128,1024]{1,0:T(8,128)(2,1)S(1)} %get-tuple-element.12), channel_id=1, source_target_pairs={{0,1},{1,2},{2,3},{3,4},{4,5},{5,6},{6,7},{7,8},{8,9},{9,10},{10,1... | collective-permute-start | bytes 786440 | tf_op jit(solution)/shard_map/ppermute | solution.py:18
  32.8 0.6 %copy-start.5 = (bf16[6,4096]{1,0:T(8,128)(2,1)}, bf16[6,4096]{1,0:T(8,128)(2,1)S(1)}, u32[]{:S(2)}) copy-start(bf16[6,4096]{1,0:T(8,128)(2,1)S(1)} %collective-permute-done.edge) | copy-start | bytes 147460
  43.7 0.7 %copy-start.4 = (bf16[128,1024]{1,0:T(8,128)(2,1)}, bf16[128,1024]{1,0:T(8,128)(2,1)S(1)}, u32[]{:S(2)}) copy-start(bf16[128,1024]{1,0:T(8,128)(2,1)S(1)} %collective-permute-done.5.halo) | copy-start | bytes 786436
  48.1 0.7 %copy-start.3 = (bf16[128,1024]{1,0:T(8,128)(2,1)}, bf16[128,1024]{1,0:T(8,128)(2,1)S(1)}, u32[]{:S(2)}) copy-start(bf16[128,1024]{1,0:T(8,128)(2,1)S(1)} %collective-permute-done.4.halo) | copy-start | bytes 786436
  52.5 0.7 %copy-start.2 = (bf16[128,1024]{1,0:T(8,128)(2,1)}, bf16[128,1024]{1,0:T(8,128)(2,1)S(1)}, u32[]{:S(2)}) copy-start(bf16[128,1024]{1,0:T(8,128)(2,1)S(1)} %collective-permute-done.3.halo) | copy-start | bytes 786436
  56.9 0.7 %copy-start.1 = (bf16[128,1024]{1,0:T(8,128)(2,1)}, bf16[128,1024]{1,0:T(8,128)(2,1)S(1)}, u32[]{:S(2)}) copy-start(bf16[128,1024]{1,0:T(8,128)(2,1)S(1)} %collective-permute-done.1.halo) | copy-start | bytes 786436

commit v2 on v0

v2 whole, which is shorter than its diff:
```python
import functools

import jax
import jax.numpy as jnp
from jax import lax
from jax.experimental import pallas as pl
from jax.experimental.pallas import tpu as pltpu
from jax.sharding import PartitionSpec as P

LANES = 128
TILE = 512
F32, BF16 = jnp.float32, jnp.bfloat16


def column(row, block):
    return jnp.transpose(jnp.broadcast_to(row, (block, block)))


def feature(x, before, taps, one, two):
    x = x.astype(F32)
    at = lax.broadcasted_iota(jnp.int32, x.shape, 0)
    far, near = before[0:1], before[1:2]
    x1 = jnp.where(at == 0, near, pltpu.roll(x, 1, 0))
    x2 = jnp.where(at == 0, far, jnp.where(at == 1, near, pltpu.roll(x, 2, 0)))
    return taps[0:1] * x + (taps[1:2] * x1) * one + (taps[2:3] * x2) * two


def kernel(axis, members, tiles, q, k, v, seg_hbm, taps_hbm, filters_hbm, bias_hbm, out,
           seg, taps, filters, bias, qb, kb, vb, pt, halo, raw, edge_send, edge, seg_prev, hrev, biasf,
           table0, table1, masks, shorts,
           small_sem, raw_sem, tail_sem, head_sem, q_sem,
           send_sem, recv_sem, small_send, small_recv):
    rows, width = q.shape
    block = filters.shape[0]
    tile = width // tiles
    per = LANES // members
    keep = block - 16
    me = lax.axis_index(axis)
    size = lax.axis_size(axis)
    has_left, has_right = me > 0, me < size - 1
    left, right = jnp.maximum(me - 1, 0), jnp.minimum(me + 1, size - 1)
    barrier = pltpu.get_barrier_semaphore()

    @pl.when(has_left)
    def _():
        pl.semaphore_signal(barrier, inc=1, device_id={axis: left}, device_id_type=pl.DeviceIdType.MESH)

    @pl.when(has_right)
    def _():
        pl.semaphore_signal(barrier, inc=1, device_id={axis: right}, device_id_type=pl.DeviceIdType.MESH)

    def cols(c):
        return pl.ds(pl.multiple_of(c * tile, tile), tile)

    def raw_copy(i):
        return pltpu.make_async_copy((q, k, v)[i].at[pl.ds(rows - 8, 8)], raw.at[i], raw_sem.at[i])

    def tail_copy(i, c):
        at = pl.ds(keep, rows - keep)
        return pltpu.make_async_copy(
            (k, v)[i].at[at, cols(c)], (kb, vb)[i].at[c, at], tail_sem.at[i, c])

    def head_copy(i, c):
        at = pl.ds(0, keep)
        return pltpu.make_async_copy(
            (k, v)[i].at[at, cols(c)], (kb, vb)[i].at[c, at], head_sem.at[i, c])

    def q_copy(c):
        return pltpu.make_async_copy(q.at[:, cols(c)], qb.at[c], q_sem.at[c])

    def remote(src, dst, s, r):
        return pltpu.make_async_remote_copy(
            src_ref=src, dst_ref=dst, send_sem=s, recv_sem=r,
            device_id={axis: right}, device_id_type=pl.DeviceIdType.MESH)

    def product_copy(c):
        return remote(pt.at[c], halo.at[c], send_sem.at[c], recv_sem.at[c])

    def edge_copy():
        return remote(edge_send, edge, small_send.at[0], small_recv.at[0])

    def seg_copy():
        return remote(seg, seg_prev, small_send.at[1], small_recv.at[1])

    small = [
        pltpu.make_async_copy(src, dst, small_sem.at[i])
        for i, (src, dst) in enumerate(
            ((seg_hbm, seg), (taps_hbm, taps), (filters_hbm, filters), (bias_hbm, bias)))
    ]
    small[0].start()
    for i in range(3):
        raw_copy(i).start()
    small[1].start()

    @pl.loop(0, tiles)
    def _(c):
        tail_copy(0, c).start()
        tail_copy(1, c).start()

    small[2].start()
    small[3].start()

    @pl.loop(0, tiles)
    def _(c):
        head_copy(0, c).start()
        head_copy(1, c).start()
        q_copy(c).start()

    tap = lax.broadcasted_iota(jnp.int32, (block, block), 0)
    lane = lax.broadcasted_iota(jnp.int32, (block, block), 1)

    def make_masks(b, row_before, row):
        own, early = column(row, block), column(row_before, block)
        one = jnp.where(tap == 0, pltpu.roll(early, 1, 0), pltpu.roll(own, 1, 0))
        two = jnp.where(tap < 2, pltpu.roll(early, 2, 0), pltpu.roll(own, 2, 0))
        shorts[b, 0] = jnp.where(own == one, 1.0, 0.0)
        shorts[b, 1] = jnp.where(own == two, 1.0, 0.0)
        masks[b, 0] = jnp.where((own == row_before) & (lane > tap), 1.0, 0.0).astype(BF16)
        masks[b, 1] = jnp.where((own == row) & (lane <= tap), 1.0, 0.0).astype(BF16)

    small[0].wait()
    seg0, seg1 = seg[0:1].astype(F32), seg[1:2].astype(F32)
    make_masks(1, seg0, seg1)
    for i in range(3):
        raw_copy(i).wait()
    edge_send[...] = jnp.concatenate(
        [raw[i].astype(F32)[6:8] for i in range(3)] + [jnp.zeros((2, width), F32)]).astype(BF16)
    for copy in small[1:]:
        copy.wait()
    turn = (tap == lax.rem(block - lane, block)).astype(BF16)
    hrev[...] = lax.dot_general(
        filters[...], turn, (((0,), (0,)), ((), ())), preferred_element_type=F32)
    biasf[...] = bias[...].astype(F32)
    pl.semaphore_wait(barrier, has_left.astype(jnp.int32) + has_right.astype(jnp.int32))

    @pl.when(has_right)
    def _():
        seg_copy().start()
        edge_copy().start()

    def part(c, s):
        return pl.ds(pl.multiple_of(c * tile + s, LANES), LANES)

    def taps_of(i, at):
        return taps[i, :, at].astype(F32)

    @pl.loop(0, tiles)
    def _(c):
        tail_copy(0, c).wait()
        tail_copy(1, c).wait()
        for s in range(0, tile, LANES):
            at, here = part(c, s), slice(s, s + LANES)
            one, two = shorts[1, 0], shorts[1, 1]
            feats = []
            for i, buf in ((1, kb), (2, vb)):
                before = buf[c, keep:block, here].astype(F32)[14:16]
                feats.append(feature(buf[c, block:, here], before, taps_of(i, at), one, two))
            pt[c, :, here] = (feats[0] * feats[1]).astype(BF16)

        @pl.when(has_right & (c > 0))
        def _():
            product_copy(jnp.maximum(c - 1, 0)).start()

    @pl.when(has_right)
    def _():
        product_copy(tiles - 1).start()

    @pl.when(has_left)
    def _():
        seg_copy().wait_recv()
        edge_copy().wait_recv()

    @pl.when(jnp.logical_not(has_left))
    def _():
        seg_prev[...] = jnp.zeros_like(seg_prev)
        edge[...] = jnp.zeros_like(edge)

        @pl.loop(0, tiles)
        def _(c):
            halo[c] = jnp.zeros_like(halo[c])

    make_masks(0, seg_prev[1:2].astype(F32), seg0)
    glane = lane // members

    @pl.loop(0, tiles)
    def _(c):
        head_copy(0, c).wait()
        head_copy(1, c).wait()
        q_copy(c).wait()

        @pl.when(has_left)
        def _():
            product_copy(c).wait_recv()

        for s in range(0, tile, LANES):
            at, here = part(c, s), slice(s, s + LANES)
            edges = edge[:, at].astype(F32)
            one, two = shorts[0, 0], shorts[0, 1]
            fk = feature(kb[c, :block, here], edges[2:4], taps_of(1, at), one, two)
            fv = feature(vb[c, :block, here], edges[4:6], taps_of(2, at), one, two)
            mid = (fk * fv).astype(BF16)
            far, near = halo[c, :, here], pt[c, :, here]
            first = (c * tile + s) // members
            for g in range(per):
                base = jnp.broadcast_to(hrev[pl.ds(first + g, 1), :], (block, block))
                ring = pltpu.roll(base, 0, 1, stride=1, stride_axis=0).astype(BF16)
                here_rows = slice(g * block, (g + 1) * block)
                table0[here_rows, :block] = ring * masks[0, 0]
                table0[here_rows, block:] = ring * masks[0, 1]
                table1[here_rows, :block] = ring * masks[1, 0]
                table1[here_rows, block:] = ring * masks[1, 1]
            brow = biasf[pl.ds((c * tile + s) // LANES, 1), :]
            for b, (table, low, high) in enumerate(((table0, far, mid), (table1, mid, near))):
                every = jnp.dot(table[...], jnp.concatenate([low, high], 0),
                                preferred_element_type=F32)
                longer = every[:block]
                for g in range(1, per):
                    longer = jnp.where(glane < g, longer, every[g * block : (g + 1) * block])
                longer = longer + brow * high.astype(F32)
                if b == 0:
                    before = edges[0:2]
                else:
                    before = qb[c, keep:block, here].astype(F32)[14:16]
                own = slice(b * block, (b + 1) * block)
                fq = feature(qb[c, own, here], before, taps_of(0, at), shorts[b, 0], shorts[b, 1])
                out[own, at] = (fq * longer).astype(BF16)

    @pl.when(has_right)
    def _():
        seg_copy().wait_send()
        edge_copy().wait_send()

        @pl.loop(0, tiles)
        def _(c):
            product_copy(c).wait_send()


def per_device(queries, keys, values, segments, short_filters, mr_filter, mr_bias):
    rows, width = queries.shape
    block, groups = mr_filter.shape
    members = width // groups
    tile = min(TILE, width)
    tiles = width // tile
    per = LANES // members
    dma = pltpu.SemaphoreType.DMA
    chunked = lambda r: pltpu.VMEM((tiles, r, tile), BF16)
    return pl.pallas_call(
        functools.partial(kernel, "tok", members, tiles),
        in_specs=[pl.BlockSpec(memory_space=pltpu.HBM)] * 7,
        out_specs=pl.BlockSpec(memory_space=pltpu.VMEM),
        out_shape=jax.ShapeDtypeStruct((rows, width), BF16),
        scratch_shapes=[
            pltpu.VMEM((rows // block, block), jnp.int32),
            pltpu.VMEM(short_filters.shape, BF16),
            pltpu.VMEM(mr_filter.shape, BF16),
            pltpu.VMEM((width // LANES, LANES), BF16),
            chunked(rows), chunked(rows), chunked(rows),
            chunked(block), chunked(block),
            pltpu.VMEM((3, 8, width), BF16),
            pltpu.VMEM((8, width), BF16),
            pltpu.VMEM((8, width), BF16),
            pltpu.VMEM((rows // block, block), jnp.int32),
            pltpu.VMEM((groups, block), F32),
            pltpu.VMEM((width // LANES, LANES), F32),
            pltpu.VMEM((per * block, 2 * block), BF16),
            pltpu.VMEM((per * block, 2 * block), BF16),
            pltpu.VMEM((2, 2, block, block), BF16),
            pltpu.VMEM((2, 2, block, block), F32),
            dma((4,)), dma((3,)), dma((2, tiles)), dma((2, tiles)), dma((tiles,)),
            dma((tiles,)), dma((tiles,)), dma((2,)), dma((2,)),
        ],
        compiler_params=pltpu.CompilerParams(collective_id=0, has_side_effects=True),
    )(queries, keys, values, segments.reshape(rows // block, block), short_filters,
      mr_filter, mr_bias.reshape(width // LANES, LANES))


def solution(mesh):
    placed = (
        P(("seq", "tok"), None),
        P(("seq", "tok"), None),
        P(("seq", "tok"), None),
        P(("seq", "tok")),
        P(),
        P(),
        P(),
    )
    return jax.shard_map(
        per_device, mesh=mesh, in_specs=placed, out_specs=P(("seq", "tok"), None), check_vma=False
    )
```

time: 260 us -> 24.2 us (0.09); the launches traced: 256 us -> 24 us
  local copies, waits for them, and re-layouts: 185 us -> 3.13 us
  other arithmetic: 39.3 us -> 0 us
  matrix products: 21.8 us -> 0 us
  Pallas kernels: 0 us -> 20.9 us
  starting transfers between devices: 9.26 us -> 0 us
    gather x2 -> x0, local copies, waits for them, and re-layouts: 152 us -> none  [long_mix(): table = flipped[:, jnp.clip(offset, 0, block - 1)]]
    dot_general x2 -> x0, matrix products: 21.8 us -> none  [one_block(): jnp.einsum('gij,jgc->igc', matrix, window, preferred_element_type=jnp.flo...]
    pallas_call x0 -> x1, Pallas kernels: none -> 20.9 us  [per_device(): pl.pallas_call(functools.partial(kernel, 'tok', members, tiles), in_specs...]
    convert_element_type x8 -> x0, other arithmetic: 16.8 us -> none  [the longest x1 8.82 us: per_device(): product_wide = (feat_k * feat_v).astype(jnp.bfloat16)]
    slice x7 -> x0, local copies, waits for them, and re-layouts: 16.3 us -> none  [the longest x2 6.38 us: long_mix(): earlier = extended[:count].reshape(blocks, block, width)]
    select_n x1 -> x0, other arithmetic: 14.2 us -> none  [long_mix(): table = jnp.where(valid[None], table, jnp.zeros((), jnp.bfloat16))]
    dynamic_update_slice x4 -> x0, local copies, waits for them, and re-layouts: 9.91 us -> none  [long_mix(): lax.map(one_block, (windows, mark_cols, mark_rows)).reshape(count, width)]
    ppermute x4 -> x0, starting transfers between devices: 9.26 us -> none  [shifted(): return lax.ppermute(value, axis, pairs)]
  transfers between devices with their start and end apart: 4 -> 0, of which waited for: 0 -> 0; matrix products, arithmetic and copies ran while one was open for 93% -> 0% of each run, Pallas kernels for 0% -> 0%
where the time goes in v2:
time: 24.2 us; the launch traced here: 24 us
  Pallas kernels  20.9 us (86%)
  local copies, waits for them, and re-layouts  3.13 us (13%)
    pallas_call x1, Pallas kernels, per_device(): pl.pallas_call(functools.partial(kernel, 'tok', members, tiles), in_specs...  20.9 us
    unnamed x1, local copies, waits for them, and re-layouts  3.13 us

profile of v2, /device:TPU:24, one launch (start us, length us, event | category | flops | bytes accessed | tf_op | source)
XLA Modules:
  0.0 24.0 jit_solution(13457732203873701712)
XLA Ops:
  0.0 20.9 %shard_map.73 = bf16[256,4096]{1,0:T(8,128)(2,1)} custom-call(bf16[256,4096]{1,0:T(8,128)(2,1)} %q.1, bf16[256,4096]{1,0:T(8,128)(2,1)} %k.1, bf16[256,4096]{1,0:T(8,128)(2,1)} %v.1, s32[2,128]{1,0:T(2,128)} %bitcast.3, bf16[3,3,4096]{2,1,0:T(4,128)(2,1)} %taps_hbm.1, bf16[128,256]{1,0:T(8,128)(2,1)} %filters_hbm.1, bf16[32,128]{1,0:T(8,128)(2,1)} %bitcast.2), custom_call_target="tpu_custom_call" | custom-call | tf_op jit(solution)/shard_map/pallas_call | solution.py:247
  20.9 3.1 %copy.9 = bf16[256,4096]{1,0:T(8,128)(2,1)} copy(bf16[256,4096]{1,0:T(8,128)(2,1)} %shard_map.73) | data formatting | bytes 4194304

commit v3 on v2

--- a/solution.py
+++ b/solution.py
@@ -248,7 +248,7 @@
         functools.partial(kernel, "tok", members, tiles),
         in_specs=[pl.BlockSpec(memory_space=pltpu.HBM)] * 7,
         out_specs=pl.BlockSpec(memory_space=pltpu.VMEM),
-        out_shape=jax.ShapeDtypeStruct((rows, width), BF16),
+        out_shape=pltpu.VMEM((rows, width), BF16),
         scratch_shapes=[
             pltpu.VMEM((rows // block, block), jnp.int32),
             pltpu.VMEM(short_filters.shape, BF16),
@@ -269,9 +269,12 @@
             dma((4,)), dma((3,)), dma((2, tiles)), dma((2, tiles)), dma((tiles,)),
             dma((tiles,)), dma((tiles,)), dma((2,)), dma((2,)),
         ],
-        compiler_params=pltpu.CompilerParams(collective_id=0, has_side_effects=True),
-    )(queries, keys, values, segments.reshape(rows // block, block), short_filters,
-      mr_filter, mr_bias.reshape(width // LANES, LANES))
+        compiler_params=pltpu.CompilerParams(
+            collective_id=0, has_side_effects=True, vmem_limit_bytes=28 * 2**20
+        ),
+    )(*(pltpu.with_memory_space_constraint(x, pltpu.HBM) for x in (
+        queries, keys, values, segments.reshape(rows // block, block), short_filters,
+        mr_filter, mr_bias.reshape(width // LANES, LANES))))
 
 
 def solution(mesh):

time: 24.2 us -> 21 us (0.87)
  local copies, waits for them, and re-layouts: 3.13 us -> 1.32 us
  Pallas kernels: 20.9 us -> 19.5 us
    unnamed x1, local copies, waits for them, and re-layouts: 3.13 us -> 1.32 us
    pallas_call x1, Pallas kernels: 20.9 us -> 19.5 us  [per_device(): pl.pallas_call(functools.partial(kernel, 'tok', members, tiles), in_specs...]
where the time goes in v3:
time: 21 us; the launch traced here: 20.8 us
  Pallas kernels  19.5 us (93%)
  local copies, waits for them, and re-layouts  1.32 us (6%)
    pallas_call x1, Pallas kernels, per_device(): pl.pallas_call(functools.partial(kernel, 'tok', members, tiles), in_specs...  19.5 us
    unnamed x1, local copies, waits for them, and re-layouts  1.32 us

profile of v3, /device:TPU:24, one launch (start us, length us, event | category | flops | bytes accessed | tf_op | source)
XLA Modules:
  0.0 20.8 jit_solution(1459270900564194258)
XLA Ops:
  0.0 19.5 %shard_map.73 = bf16[256,4096]{1,0:T(8,128)(2,1)S(1)} custom-call(bf16[256,4096]{1,0:T(8,128)(2,1)} %q.1, bf16[256,4096]{1,0:T(8,128)(2,1)} %k.1, bf16[256,4096]{1,0:T(8,128)(2,1)} %v.1, s32[2,128]{1,0:T(2,128)} %bitcast.3, bf16[3,3,4096]{2,1,0:T(4,128)(2,1)} %taps_hbm.1, bf16[128,256]{1,0:T(8,128)(2,1)} %filters_hbm.1, bf16[32,128]{1,0:T(8,128)(2,1)} %bitcast.2), custom_call_target="tpu_custom_call" | custom-call | tf_op jit(solution)/shard_map/pallas_call | solution.py:247
  19.5 1.3 %copy.9 = bf16[256,4096]{1,0:T(8,128)(2,1)} copy(bf16[256,4096]{1,0:T(8,128)(2,1)S(1)} %shard_map.73) | data formatting | bytes 4194304

commit v4 on v3

--- a/solution.py
+++ b/solution.py
@@ -27,7 +27,7 @@
 
 def kernel(axis, members, tiles, q, k, v, seg_hbm, taps_hbm, filters_hbm, bias_hbm, out,
            seg, taps, filters, bias, qb, kb, vb, pt, halo, raw, edge_send, edge, seg_prev, hrev, biasf,
-           table0, table1, masks, shorts,
+           table0, table1, picked, masks, shorts,
            small_sem, raw_sem, tail_sem, head_sem, q_sem,
            send_sem, recv_sem, small_send, small_recv):
     rows, width = q.shape
@@ -125,12 +125,6 @@
         raw_copy(i).wait()
     edge_send[...] = jnp.concatenate(
         [raw[i].astype(F32)[6:8] for i in range(3)] + [jnp.zeros((2, width), F32)]).astype(BF16)
-    for copy in small[1:]:
-        copy.wait()
-    turn = (tap == lax.rem(block - lane, block)).astype(BF16)
-    hrev[...] = lax.dot_general(
-        filters[...], turn, (((0,), (0,)), ((), ())), preferred_element_type=F32)
-    biasf[...] = bias[...].astype(F32)
     pl.semaphore_wait(barrier, has_left.astype(jnp.int32) + has_right.astype(jnp.int32))
 
     @pl.when(has_right)
@@ -143,6 +137,8 @@
 
     def taps_of(i, at):
         return taps[i, :, at].astype(F32)
+
+    small[1].wait()
 
     @pl.loop(0, tiles)
     def _(c):
@@ -164,6 +160,13 @@
     @pl.when(has_right)
     def _():
         product_copy(tiles - 1).start()
+
+    small[2].wait()
+    small[3].wait()
+    turn = (tap == lax.rem(block - lane, block)).astype(BF16)
+    hrev[...] = lax.dot_general(
+        filters[...], turn, (((0,), (0,)), ((), ())), preferred_element_type=F32)
+    biasf[...] = bias[...].astype(F32)
 
     @pl.when(has_left)
     def _():
@@ -213,10 +216,9 @@
             for b, (table, low, high) in enumerate(((table0, far, mid), (table1, mid, near))):
                 every = jnp.dot(table[...], jnp.concatenate([low, high], 0),
                                 preferred_element_type=F32)
-                longer = every[:block]
-                for g in range(1, per):
-                    longer = jnp.where(glane < g, longer, every[g * block : (g + 1) * block])
-                longer = longer + brow * high.astype(F32)
+                for g in range(per):
+                    pltpu.store(picked.at[b], every[g * block : (g + 1) * block], mask=glane == g)
+                longer = picked[b] + brow * high.astype(F32)
                 if b == 0:
                     before = edges[0:2]
                 else:
@@ -264,6 +266,7 @@
             pltpu.VMEM((width // LANES, LANES), F32),
             pltpu.VMEM((per * block, 2 * block), BF16),
             pltpu.VMEM((per * block, 2 * block), BF16),
+            pltpu.VMEM((2, block, LANES), F32),
             pltpu.VMEM((2, 2, block, block), BF16),
             pltpu.VMEM((2, 2, block, block), F32),
             dma((4,)), dma((3,)), dma((2, tiles)), dma((2, tiles)), dma((tiles,)),

time: 21 us -> 20.2 us (0.962)
  Pallas kernels: 19.5 us -> 18.8 us
    pallas_call x1, Pallas kernels: 19.5 us -> 18.8 us  [per_device(): pl.pallas_call(functools.partial(kernel, 'tok', members, tiles), in_specs...]
where the time goes in v4:
time: 20.2 us; the launch traced here: 20.1 us
  Pallas kernels  18.8 us (93%)
  local copies, waits for them, and re-layouts  1.32 us (7%)
    pallas_call x1, Pallas kernels, per_device(): pl.pallas_call(functools.partial(kernel, 'tok', members, tiles), in_specs...  18.8 us
    unnamed x1, local copies, waits for them, and re-layouts  1.32 us

profile of v4, /device:TPU:24, one launch (start us, length us, event | category | flops | bytes accessed | tf_op | source)
XLA Modules:
  0.0 20.1 jit_solution(5397735979883319380)
XLA Ops:
  0.0 18.8 %shard_map.73 = bf16[256,4096]{1,0:T(8,128)(2,1)S(1)} custom-call(bf16[256,4096]{1,0:T(8,128)(2,1)} %q.1, bf16[256,4096]{1,0:T(8,128)(2,1)} %k.1, bf16[256,4096]{1,0:T(8,128)(2,1)} %v.1, s32[2,128]{1,0:T(2,128)} %bitcast.3, bf16[3,3,4096]{2,1,0:T(4,128)(2,1)} %taps_hbm.1, bf16[128,256]{1,0:T(8,128)(2,1)} %filters_hbm.1, bf16[32,128]{1,0:T(8,128)(2,1)} %bitcast.2), custom_call_target="tpu_custom_call" | custom-call | tf_op jit(solution)/shard_map/pallas_call | solution.py:249
  18.8 1.3 %copy.9 = bf16[256,4096]{1,0:T(8,128)(2,1)} copy(bf16[256,4096]{1,0:T(8,128)(2,1)S(1)} %shard_map.73) | data formatting | bytes 4194304

commit v5 on v4

--- a/solution.py
+++ b/solution.py
@@ -120,7 +120,6 @@
 
     small[0].wait()
     seg0, seg1 = seg[0:1].astype(F32), seg[1:2].astype(F32)
-    make_masks(1, seg0, seg1)
     for i in range(3):
         raw_copy(i).wait()
     edge_send[...] = jnp.concatenate(
@@ -131,6 +130,8 @@
     def _():
         seg_copy().start()
         edge_copy().start()
+
+    make_masks(1, seg0, seg1)
 
     def part(c, s):
         return pl.ds(pl.multiple_of(c * tile + s, LANES), LANES)

time: 20.2 us -> 20.3 us (level)
  no operation moved by 1% of the time
where the time goes in v5:
time: 20.3 us; the launch traced here: 20.1 us
  Pallas kernels  18.8 us (93%)
  local copies, waits for them, and re-layouts  1.32 us (7%)
    pallas_call x1, Pallas kernels, per_device(): pl.pallas_call(functools.partial(kernel, 'tok', members, tiles), in_specs...  18.8 us
    unnamed x1, local copies, waits for them, and re-layouts  1.32 us

profile of v5, /device:TPU:24, one launch (start us, length us, event | category | flops | bytes accessed | tf_op | source)
XLA Modules:
  0.0 20.1 jit_solution(16580246745236320249)
XLA Ops:
  0.0 18.8 %shard_map.73 = bf16[256,4096]{1,0:T(8,128)(2,1)S(1)} custom-call(bf16[256,4096]{1,0:T(8,128)(2,1)} %q.1, bf16[256,4096]{1,0:T(8,128)(2,1)} %k.1, bf16[256,4096]{1,0:T(8,128)(2,1)} %v.1, s32[2,128]{1,0:T(2,128)} %bitcast.3, bf16[3,3,4096]{2,1,0:T(4,128)(2,1)} %taps_hbm.1, bf16[128,256]{1,0:T(8,128)(2,1)} %filters_hbm.1, bf16[32,128]{1,0:T(8,128)(2,1)} %bitcast.2), custom_call_target="tpu_custom_call" | custom-call | tf_op jit(solution)/shard_map/pallas_call | solution.py:250
  18.8 1.3 %copy.9 = bf16[256,4096]{1,0:T(8,128)(2,1)} copy(bf16[256,4096]{1,0:T(8,128)(2,1)S(1)} %shard_map.73) | data formatting | bytes 4194304

commit v6 on v5

--- a/solution.py
+++ b/solution.py
@@ -153,10 +153,11 @@
                 before = buf[c, keep:block, here].astype(F32)[14:16]
                 feats.append(feature(buf[c, block:, here], before, taps_of(i, at), one, two))
             pt[c, :, here] = (feats[0] * feats[1]).astype(BF16)
-
-        @pl.when(has_right & (c > 0))
-        def _():
-            product_copy(jnp.maximum(c - 1, 0)).start()
+            if s == 0:
+                @pl.when(has_right & (c > 0))
+                def _():
+                    product_copy(jnp.maximum(c - 1, 0)).start()
+
 
     @pl.when(has_right)
     def _():

time: 20.3 us -> 20.3 us (level)
  no operation moved by 1% of the time
where the time goes in v6:
time: 20.3 us; the launch traced here: 20.1 us
  Pallas kernels  18.8 us (93%)
  local copies, waits for them, and re-layouts  1.32 us (7%)
    pallas_call x1, Pallas kernels, per_device(): pl.pallas_call(functools.partial(kernel, 'tok', members, tiles), in_specs...  18.8 us
    unnamed x1, local copies, waits for them, and re-layouts  1.32 us

profile of v6, /device:TPU:24, one launch (start us, length us, event | category | flops | bytes accessed | tf_op | source)
XLA Modules:
  0.0 20.1 jit_solution(6429707018585667102)
XLA Ops:
  0.0 18.8 %shard_map.73 = bf16[256,4096]{1,0:T(8,128)(2,1)S(1)} custom-call(bf16[256,4096]{1,0:T(8,128)(2,1)} %q.1, bf16[256,4096]{1,0:T(8,128)(2,1)} %k.1, bf16[256,4096]{1,0:T(8,128)(2,1)} %v.1, s32[2,128]{1,0:T(2,128)} %bitcast.3, bf16[3,3,4096]{2,1,0:T(4,128)(2,1)} %taps_hbm.1, bf16[128,256]{1,0:T(8,128)(2,1)} %filters_hbm.1, bf16[32,128]{1,0:T(8,128)(2,1)} %bitcast.2), custom_call_target="tpu_custom_call" | custom-call | tf_op jit(solution)/shard_map/pallas_call | solution.py:251
  18.8 1.3 %copy.9 = bf16[256,4096]{1,0:T(8,128)(2,1)} copy(bf16[256,4096]{1,0:T(8,128)(2,1)S(1)} %shard_map.73) | data formatting | bytes 4194304
